TPU v7x, 256 devices: a whole 4x4x8 slice. The times are simulated.
256 devices in a mesh: seq: 64 (over x, z, core), ch: 4 (over y).
Axes of the slice: x: 4, y: 4, z: 8, core: 2. Of those that a mesh axis runs over, the one named last changes fastest.
Arguments:
- gate_rows: bfloat16 [32768, 2048], P(('seq', 'ch')), may hold values from -6 to 6
- key_rows: bfloat16 [32768, 2048], P(('seq', 'ch')), may hold values from -6 to 6
- value_rows: bfloat16 [32768, 2048], P(('seq', 'ch')), may hold values from -6 to 6
- spectrum: float32 [2, 128, 512, 2048], P(None, 'seq', None, 'ch'), may hold values from -6 to 6
- skip_bias: float32 [2048], replicated, may hold values from -1 to 1
Outputs:
- gated: bfloat16 [32768, 2048], P(('seq', 'ch'))
All inputs are finite; a program needn't handle non-finite values.
Results may differ from a plain program's by a relative error of at most 0.0049.
Values may be sent and summed in bfloat16 or wider, within the bound.
A program may use at most 128 MiB of HBM per device.

v0:
```python
import math
import jax
import jax.numpy as jnp
import numpy as np
from jax import lax
from jax.sharding import PartitionSpec as P

f32, bf16 = (jnp.float32, jnp.bfloat16)


def phase_table(first, second, modulus):
    turns = first[:, None] * second[None, :] % modulus
    angles = turns.astype(f32) * (2.0 * math.pi / modulus)
    return (jnp.cos(angles), jnp.sin(angles))


def dot(eq, a, b):
    return jnp.einsum(eq, a.astype(bf16), b.astype(bf16), preferred_element_type=f32)


def convolve(product, spectrum):
    seq_count = lax.axis_size("seq")
    tokens, width = product.shape
    length_two = 2 * seq_count * tokens
    offsets = jnp.arange(2 * seq_count, dtype=jnp.int32)
    places = jnp.arange(seq_count, dtype=jnp.int32)
    residues = jnp.arange(tokens, dtype=jnp.int32)
    off_cos, off_sin = phase_table(offsets, places, 2 * seq_count)
    res_cos, res_sin = phase_table(residues, residues, tokens)
    block = tokens // seq_count
    device = lax.axis_index("seq")
    values = lax.all_to_all(
        product.reshape(1, tokens, width), "seq", split_axis=1, concat_axis=0, tiled=True
    )
    off = jnp.stack([off_cos, -off_sin], 1)
    part = dot("kip,prc->kirc", off, values)
    own_rows = device * block + jnp.arange(block, dtype=jnp.int32)
    tw_cos, tw_sin = phase_table(offsets, own_rows, length_two)
    tw_cos = tw_cos[:, :, None]
    tw_sin = tw_sin[:, :, None]
    part = jnp.stack(
        [part[:, 0] * tw_cos + part[:, 1] * tw_sin, part[:, 1] * tw_cos - part[:, 0] * tw_sin], 1
    )
    part = lax.all_to_all(part.astype(bf16), "seq", split_axis=0, concat_axis=2, tiled=True)
    table = jnp.stack([jnp.stack([res_cos, res_sin], 0), jnp.stack([-res_sin, res_cos], 0)], 0)
    nxt = dot("oisr,girc->gosc", table, part)
    re, im = (nxt[:, 0], nxt[:, 1])
    spec_real, spec_imag = (spectrum[0], spectrum[1])
    filt = jnp.stack([re * spec_real - im * spec_imag, re * spec_imag + im * spec_real], 1)
    back = dot("oisr,gosc->girc", table, filt)
    own_offsets = 2 * device + jnp.arange(2, dtype=jnp.int32)
    un_cos, un_sin = phase_table(own_offsets, residues, length_two)
    un_cos = un_cos[:, :, None]
    un_sin = un_sin[:, :, None]
    back = jnp.stack(
        [back[:, 0] * un_cos - back[:, 1] * un_sin, back[:, 1] * un_cos + back[:, 0] * un_sin], 1
    )
    back = lax.all_to_all(back.astype(bf16), "seq", split_axis=2, concat_axis=0, tiled=True)
    field = dot("kip,kirc->prc", off, back) / length_two
    field = lax.all_to_all(field.astype(bf16), "seq", split_axis=0, concat_axis=1, tiled=True)
    return field.reshape(tokens, width)


def per_device(gate_rows, key_rows, value_rows, spectrum, skip_bias):
    product = (key_rows.astype(f32) * value_rows.astype(f32)).astype(bf16)
    cols = lax.all_to_all(product, "ch", split_axis=1, concat_axis=0, tiled=True)
    field = convolve(cols, spectrum)
    field = lax.all_to_all(field, "ch", split_axis=0, concat_axis=1, tiled=True)
    gated = gate_rows.astype(f32) * (field.astype(f32) + skip_bias[None, :] * product.astype(f32))
    return gated.astype(bf16)


def solution(mesh):
    placed = (
        P(("seq", "ch"), None),
        P(("seq", "ch"), None),
        P(("seq", "ch"), None),
        P(None, "seq", None, "ch"),
        P(),
    )
    return jax.shard_map(
        per_device, mesh=mesh, in_specs=placed, out_specs=P(("seq", "ch"), None), check_vma=False
    )
```

profile of v0, /device:TPU:1, one launch (start us, length us, event | category | flops | bytes accessed | tf_op | source)
XLA Modules:
  0.0 231.2 jit_solution(8587661304348707398)
XLA Ops:
  0.0 1.3 copy.53
  1.3 1.3 copy.54
  2.6 0.1 multiply_convert_fusion
  2.8 13.4 %all_to_all.86 = bf16[128,4,512]{0,2,1:T(8,128)(2,1)S(1)} all-to-all(bf16[128,4,512]{0,2,1:T(8,128)(2,1)S(1)} %bitcast.98), channel_id=1, replica_groups=mesh['seq'=64,'ch'=4] {'ch'}, dimensions={1} | all-to-all | bytes 1048576 | tf_op jit(solution)/shard_map/all_to_all | solution.py:66
  16.2 0.2 copy.55
  16.4 0.8 copy.98
  17.2 0.5 broadcast.368
  17.7 3.8 %reduce = bf16[512,512]{1,0:T(8,128)(2,1)S(1)} reduce(bf16[512,1,512]{2,1,0:T(2,128)(2,1)S(1)} %bitcast.100, bf16[]{:T(256)} %broadcast.368), dimensions={1}, to_apply=%bitcast.96.reduce_sub_computation | reduce | bytes 1048578
  21.5 1.0 reshape.296
  22.5 13.3 %all-to-all-start.1 = ((bf16[64,2,2048]{2,1,0:T(2,128)(2,1)}), bf16[64,2,2048]{2,1,0:T(2,128)(2,1)S(1)}, u32[]{:S(2)}, u32[]{:S(2)}) async-start(bf16[64,2,2048]{2,1,0:T(2,128)(2,1)} %reshape.296), calls=%async_computation.1 | async-start | bytes 1048576 | tf_op jit(solution)/shard_map/all_to_all | solution.py:32
  35.9 0.2 negate_convert_fusion.1
  36.2 17.0 %all-to-all-done.1 = bf16[64,2,2048]{2,1,0:T(2,128)(2,1)S(1)} async-done(((bf16[64,2,2048]{2,1,0:T(2,128)(2,1)}), bf16[64,2,2048]{2,1,0:T(2,128)(2,1)S(1)}, u32[]{:S(2)}, u32[]{:S(2)}) %all-to-all-start.1) | async-done | bytes 524320 | tf_op jit(solution)/shard_map/all_to_all | solution.py:32
  53.2 0.5 reshape.297
  53.7 0.1 copy.97
  53.9 0.7 fusion.21
  54.6 0.6 add_convert_fusion.1
  55.2 0.2 pad_maximum_fusion
  55.4 2.5 %copy.58 = bf16[128,2,8,512]{3,2,1,0:T(8,128)(2,1)} copy(bf16[128,2,8,512]{3,0,2,1:T(8,128)(2,1)S(1)} %pad_maximum_fusion) | data formatting | bytes 4194304 | tf_op jit(solution)/shard_map/stack | solution.py:41
  57.9 6.5 %all-to-all-start.2 = ((bf16[128,2,8,512]{3,2,1,0:T(8,128)(2,1)}), bf16[128,2,8,512]{3,2,1,0:T(8,128)(2,1)}, u32[]{:S(2)}, u32[]{:S(2)}) async-start(bf16[128,2,8,512]{3,2,1,0:T(8,128)(2,1)} %copy.58), calls=%async_computation.2 | async-start | bytes 4194304 | tf_op jit(solution)/shard_map/all_to_all | solution.py:44
  64.4 4.6 %fusion.50 = (f32[1,2,512,512]{3,2,1,0:T(8,128)}, f32[1,2,512,512]{3,2,1,0:T(8,128)}) fusion(f32[2,2,512,512]{3,2,1,0:T(8,128)} %param.8), kind=kLoop, calls=%fused_computation.91 | loop fusion | bytes 8388608 | tf_op jit(solution)/shard_map/slice | solution.py:48
  69.0 1.9 copy.79
  71.0 2.9 %copy.80 = f32[1,2,512,512]{2,3,1,0:T(8,128)} copy(f32[1,2,512,512]{3,2,1,0:T(8,128)} %get-tuple-element.12) | data formatting | bytes 4194304
  73.9 4.0 %fusion.25 = bf16[1,512,512]{2,1,0:T(8,128)(2,1)S(1)} fusion(), kind=kLoop, calls=%fused_computation.52 | loop fusion | flops 3932160 | bytes 524288 | tf_op jit(solution)/shard_map/convert.13
  77.8 4.3 %negate_convert_fusion = (bf16[1,512,512]{2,1,0:T(8,128)(2,1)S(1)}, bf16[1,512,512]{2,1,0:T(8,128)(2,1)S(1)}) fusion(), kind=kLoop, calls=%fused_computation.41 | loop fusion | flops 4456448 | bytes 1048576 | tf_op jit(solution)/shard_map/convert.9
  82.2 1.5 maximum_bitcast_fusion.2
  83.7 0.2 fusion.44
  83.9 31.6 %all-to-all-done.2 = bf16[128,2,8,512]{3,2,1,0:T(8,128)(2,1)} async-done(((bf16[128,2,8,512]{3,2,1,0:T(8,128)(2,1)}), bf16[128,2,8,512]{3,2,1,0:T(8,128)(2,1)}, u32[]{:S(2)}, u32[]{:S(2)}) %all-to-all-start.2) | async-done | bytes 2097184 | tf_op jit(solution)/shard_map/all_to_all | solution.py:44
  115.5 4.7 %convolution_bitcast_fusion.1 = f32[2,2,512,512]{2,3,1,0:T(8,128)S(1)} fusion(bf16[2,2,64,8,512]{4,3,1,0,2:T(8,128)(2,1)} %bitcast.7, bf16[1,2,512,512]{3,2,1,0:T(8,128)(2,1)} %get-tuple-element.14, bf16[1,2,512,512]{3,2,1,0:T(8,128)(2,1)} %get-tuple-element.13), kind=kOutput, calls=%fused_computation.1 | convolution fusion | flops 2151677952 | bytes 8388608 | tf_op jit(solution)/shard_map/oisr,girc->gosc/dot_general | solution.py:18
  120.3 1.2 fusion.5
  121.5 0.3 copy-done.2
  121.8 2.3 %convolution_bitcast_fusion = f32[2,2,512,512]{2,3,1,0:T(8,128)S(1)} fusion(bf16[2,1,512,512]{2,3,1,0:T(8,128)(2,1)S(1)} %get-tuple-element.6, bf16[2,1,512,512]{2,3,1,0:T(8,128)(2,1)S(1)} %get-tuple-element.5, bf16[1,2,512,512]{3,2,1,0:T(8,128)(2,1)S(1)} %copy-done.2, bf16[1,2,512,512]{3,2,1,0:T(8,128)(2,1)S(1)} %copy-done.1), kind=kOutput, calls=%fused_computation | convolution fusion | flops 2152726528 | bytes 8388608 | tf_op jit(solution)/shard_map/oisr,gosc->girc/dot_general | solution.py:18
  124.1 0.7 subtract_convert_fusion
  124.8 0.2 pad_maximum_fusion.2
  125.0 4.0 %copy.64 = bf16[2,2,512,512]{3,1,0,2:T(2,128)(2,1)} copy(bf16[2,2,512,512]{2,3,1,0:T(8,128)(2,1)S(1)} %pad_maximum_fusion.2) | data formatting | bytes 4194304 | tf_op jit(solution)/shard_map/stack | solution.py:55
  129.1 57.1 %all_to_all.87 = bf16[2,2,512,512]{3,1,0,2:T(2,128)(2,1)S(1)} all-to-all(bf16[2,2,512,512]{3,1,0,2:T(2,128)(2,1)} %copy.64), channel_id=1, replica_groups=mesh['seq'=64,'ch'=4] {'seq'}, dimensions={2} | all-to-all | bytes 4194304 | tf_op jit(solution)/shard_map/all_to_all | solution.py:58
  186.1 0.4 copy.96
  186.6 3.5 %copy.66 = bf16[64,2,2,8,512]{4,1,0,2,3:T(2,128)(2,1)} copy(bf16[64,2,2,8,512]{4,3,0,2,1:T(8,128)(2,1)S(1)} %bitcast.97) | data formatting | bytes 4194304 | tf_op jit(solution)/shard_map/all_to_all | solution.py:58
  190.1 2.7 %all_to_all.76 = bf16[128,2,8,512]{3,0,1,2:T(8,128)(2,1)S(1)} reshape(bf16[64,2,2,8,512]{4,1,0,2,3:T(2,128)(2,1)} %copy.66) | data formatting | bytes 4194304 | tf_op jit(solution)/shard_map/all_to_all | solution.py:58
  192.8 0.5 fusion.12
  193.3 0.3 copy.67
  193.6 23.0 %all_to_all.88 = bf16[64,8,512]{2,1,0:T(8,128)(2,1)} all-to-all(bf16[64,8,512]{2,1,0:T(8,128)(2,1)S(1)} %copy.67), channel_id=1, replica_groups=mesh['seq'=64,'ch'=4] {'seq'}, dimensions={0} | all-to-all | bytes 1048576 | tf_op jit(solution)/shard_map/all_to_all | solution.py:60
  216.7 3.5 %all-to-all-start.5 = ((bf16[4,128,512]{2,1,0:T(8,128)(2,1)}), bf16[4,128,512]{2,1,0:T(8,128)(2,1)S(1)}, u32[]{:S(2)}, u32[]{:S(2)}) async-start(bf16[4,128,512]{2,1,0:T(8,128)(2,1)} %bitcast.30), calls=%async_computation.5 | async-start | bytes 1048576 | tf_op jit(solution)/shard_map/all_to_all | solution.py:68
  220.1 0.3 copy.52
  220.4 9.0 %all-to-all-done.5 = bf16[4,128,512]{2,1,0:T(8,128)(2,1)S(1)} async-done(((bf16[4,128,512]{2,1,0:T(8,128)(2,1)}), bf16[4,128,512]{2,1,0:T(8,128)(2,1)S(1)}, u32[]{:S(2)}, u32[]{:S(2)}) %all-to-all-start.5) | async-done | bytes 524320 | tf_op jit(solution)/shard_map/all_to_all | solution.py:68
  229.4 0.1 convert_bitcast_fusion
  229.5 0.3 copy.68
  229.9 0.3 fusion.17
  230.2 1.0 copy.69
  (12 shorter events, 0.1 us)
Async XLA Ops:
  22.5 30.7 %all-to-all-start.1 = ((bf16[64,2,2048]{2,1,0:T(2,128)(2,1)}), bf16[64,2,2048]{2,1,0:T(2,128)(2,1)S(1)}, u32[]{:S(2)}, u32[]{:S(2)}) async-start(bf16[64,2,2048]{2,1,0:T(2,128)(2,1)} %reshape.296), calls=%async_computation.1 | async-start | bytes 1048576 | tf_op jit(solution)/shard_map/all_to_all | solution.py:32
  57.9 57.6 %all-to-all-start.2 = ((bf16[128,2,8,512]{3,2,1,0:T(8,128)(2,1)}), bf16[128,2,8,512]{3,2,1,0:T(8,128)(2,1)}, u32[]{:S(2)}, u32[]{:S(2)}) async-start(bf16[128,2,8,512]{3,2,1,0:T(8,128)(2,1)} %copy.58), calls=%async_computation.2 | async-start | bytes 4194304 | tf_op jit(solution)/shard_map/all_to_all | solution.py:44
  115.5 4.7 %copy-start = (f32[1,2,512,512]{2,3,1,0:T(8,128)S(1)}, f32[1,2,512,512]{2,3,1,0:T(8,128)}, u32[]{:S(2)}) copy-start(f32[1,2,512,512]{2,3,1,0:T(8,128)} %copy.80) | copy-start | bytes 6291460
  120.3 1.2 copy-start.1
  120.3 1.5 copy-start.2
  193.3 26.8 %copy-start.3 = (bf16[128,2048]{1,0:T(8,128)(2,1)S(1)}, bf16[128,2048]{1,0:T(8,128)(2,1)}, u32[]{:S(2)}) copy-start(bf16[128,2048]{1,0:T(8,128)(2,1)} %param.5) | copy-start | bytes 1572868
  216.7 12.7 %all-to-all-start.5 = ((bf16[4,128,512]{2,1,0:T(8,128)(2,1)}), bf16[4,128,512]{2,1,0:T(8,128)(2,1)S(1)}, u32[]{:S(2)}, u32[]{:S(2)}) async-start(bf16[4,128,512]{2,1,0:T(8,128)(2,1)} %bitcast.30), calls=%async_computation.5 | async-start | bytes 1048576 | tf_op jit(solution)/shard_map/all_to_all | solution.py:68
  220.4 9.4 %copy-start.4 = (f32[2048]{0:T(1024)S(1)}, f32[2048]{0:T(1024)}, u32[]{:S(2)}) copy-start(f32[2048]{0:T(1024)} %param.9) | copy-start | bytes 24580
where the time goes:
time: 232 us; the launch traced here: 231 us
  blocking collectives  93.5 us (40%)
  waiting for transfers between devices  57.6 us (25%)
  local copies, waits for them, and re-layouts  30.7 us (13%)
  starting transfers between devices  23.3 us (10%)
  other arithmetic  17.6 us (8%)
  matrix products  8.25 us (4%)
    all_to_all x1, blocking collectives, convolve(): lax.all_to_all(back.astype(bf16), 'seq', split_axis=2, concat_axis=0, til...  57.1 us
    all_to_all x1, waiting for transfers between devices, convolve(): lax.all_to_all(part.astype(bf16), 'seq', split_axis=0, concat_axis=2, til...  31.6 us
    all_to_all x1, blocking collectives, convolve(): lax.all_to_all(field.astype(bf16), 'seq', split_axis=0, concat_axis=1, ti...  23 us
    all_to_all x1, waiting for transfers between devices, convolve(): lax.all_to_all(product.reshape(1, tokens, width), 'seq', split_axis=1, co...  17 us
    all_to_all x1, blocking collectives, per_device(): lax.all_to_all(product, 'ch', split_axis=1, concat_axis=0, tiled=True)  13.4 us
    all_to_all x1, starting transfers between devices, convolve(): lax.all_to_all(product.reshape(1, tokens, width), 'seq', split_axis=1, co...  13.3 us
    another operation x6, other arithmetic  11 us
    unnamed x19, local copies, waits for them, and re-layouts  10.2 us
  transfers between devices with their start and end apart: 3, of which 3 were waited for; matrix products, arithmetic and copies ran while one was open for 9% of the time, Pallas kernels for 0%

commit v1 on v0

--- a/solution.py
+++ b/solution.py
@@ -55,7 +55,12 @@
     back = jnp.stack(
         [back[:, 0] * un_cos - back[:, 1] * un_sin, back[:, 1] * un_cos + back[:, 0] * un_sin], 1
     )
-    back = lax.all_to_all(back.astype(bf16), "seq", split_axis=2, concat_axis=0, tiled=True)
+    back = jnp.concatenate(
+        lax.all_to_all(
+            jnp.stack(jnp.split(back.astype(bf16), lax.axis_size("seq"), axis=2)), "seq", 0, 0
+        ),
+        axis=0,
+    )
     field = dot("kip,kirc->prc", off, back) / length_two
     field = lax.all_to_all(field.astype(bf16), "seq", split_axis=0, concat_axis=1, tiled=True)
     return field.reshape(tokens, width)

time: 232 us -> 223 us (0.961)
  local copies, waits for them, and re-layouts: 30.7 us -> 20 us
    all_to_all x3 -> x0, local copies, waits for them, and re-layouts: 6.65 us -> none  [convolve(): lax.all_to_all(back.astype(bf16), 'seq', split_axis=2, concat_axis=0, til...]
    another operation x1 -> x0, local copies, waits for them, and re-layouts: 4.04 us -> none  [convolve(): jnp.stack([back[:, 0] * un_cos - back[:, 1] * un_sin, back[:, 1] * un_cos...]
where the time goes in v1:
time: 223 us
  blocking collectives  93.3 us (42%)
  waiting for transfers between devices  57.6 us (26%)
  starting transfers between devices  23.3 us (10%)
  local copies, waits for them, and re-layouts  20 us (9%)
  other arithmetic  17.5 us (8%)
  matrix products  10.3 us (5%)
    all_to_all x1, blocking collectives, convolve(): lax.all_to_all(jnp.stack(jnp.split(back.astype(bf16), lax.axis_size('seq'...  56.9 us
    all_to_all x1, waiting for transfers between devices, convolve(): lax.all_to_all(part.astype(bf16), 'seq', split_axis=0, concat_axis=2, til...  31.6 us
    all_to_all x1, blocking collectives, convolve(): lax.all_to_all(field.astype(bf16), 'seq', split_axis=0, concat_axis=1, ti...  23 us
    all_to_all x1, waiting for transfers between devices, convolve(): lax.all_to_all(product.reshape(1, tokens, width), 'seq', split_axis=1, co...  17 us
    all_to_all x1, blocking collectives, per_device(): lax.all_to_all(product, 'ch', split_axis=1, concat_axis=0, tiled=True)  13.4 us
    all_to_all x1, starting transfers between devices, convolve(): lax.all_to_all(product.reshape(1, tokens, width), 'seq', split_axis=1, co...  13.3 us
    another operation x6, other arithmetic  10.8 us
    dot_general x4, matrix products, dot(): jnp.einsum(eq, a.astype(bf16), b.astype(bf16), preferred_element_type=f32)  10.3 us
  transfers between devices with their start and end apart: 3, of which 3 were waited for; matrix products, arithmetic and copies ran while one was open for 9% of the time, Pallas kernels for 0%

profile of v1, /device:TPU:1, one launch (start us, length us, event | category | flops | bytes accessed | tf_op | source)
XLA Modules:
  0.0 222.8 jit_solution(7081471842509237084)
XLA Ops:
  0.0 1.3 copy.53
  1.3 1.3 copy.54
  2.6 0.1 multiply_convert_fusion
  2.8 13.4 %all_to_all.73 = bf16[128,4,512]{0,2,1:T(8,128)(2,1)S(1)} all-to-all(bf16[128,4,512]{0,2,1:T(8,128)(2,1)S(1)} %bitcast.223), channel_id=1, replica_groups=mesh['seq'=64,'ch'=4] {'ch'}, dimensions={1} | all-to-all | bytes 1048576 | tf_op jit(solution)/shard_map/all_to_all | solution.py:71
  16.2 0.2 copy.55
  16.4 0.8 copy.104
  17.2 0.5 broadcast.368
  17.7 3.8 %reduce = bf16[512,512]{1,0:T(8,128)(2,1)S(1)} reduce(bf16[512,1,512]{2,1,0:T(2,128)(2,1)S(1)} %bitcast.225, bf16[]{:T(256)} %broadcast.368), dimensions={1}, to_apply=%bitcast.222.reduce_sub_computation | reduce | bytes 1048578
  21.5 1.0 reshape.300
  22.5 13.3 %all-to-all-start.1 = ((bf16[64,2,2048]{2,1,0:T(2,128)(2,1)}), bf16[64,2,2048]{2,1,0:T(2,128)(2,1)S(1)}, u32[]{:S(2)}, u32[]{:S(2)}) async-start(bf16[64,2,2048]{2,1,0:T(2,128)(2,1)} %reshape.300), calls=%async_computation.1 | async-start | bytes 1048576 | tf_op jit(solution)/shard_map/all_to_all | solution.py:32
  35.9 0.2 negate_convert_fusion.1
  36.1 0.1 fusion.118
  36.2 17.0 %all-to-all-done.1 = bf16[64,2,2048]{2,1,0:T(2,128)(2,1)S(1)} async-done(((bf16[64,2,2048]{2,1,0:T(2,128)(2,1)}), bf16[64,2,2048]{2,1,0:T(2,128)(2,1)S(1)}, u32[]{:S(2)}, u32[]{:S(2)}) %all-to-all-start.1) | async-done | bytes 524320 | tf_op jit(solution)/shard_map/all_to_all | solution.py:32
  53.2 0.5 reshape.301
  53.7 0.1 copy.103
  53.9 0.7 fusion.29
  54.6 0.6 add_convert_fusion.1
  55.2 0.2 pad_maximum_fusion
  55.4 2.5 %copy.58 = bf16[128,2,8,512]{3,2,1,0:T(8,128)(2,1)} copy(bf16[128,2,8,512]{3,0,2,1:T(8,128)(2,1)S(1)} %pad_maximum_fusion) | data formatting | bytes 4194304 | tf_op jit(solution)/shard_map/stack | solution.py:41
  57.9 6.5 %all-to-all-start.2 = ((bf16[128,2,8,512]{3,2,1,0:T(8,128)(2,1)}), bf16[128,2,8,512]{3,2,1,0:T(8,128)(2,1)}, u32[]{:S(2)}, u32[]{:S(2)}) async-start(bf16[128,2,8,512]{3,2,1,0:T(8,128)(2,1)} %copy.58), calls=%async_computation.2 | async-start | bytes 4194304 | tf_op jit(solution)/shard_map/all_to_all | solution.py:44
  64.4 4.6 %fusion.123 = (f32[1,2,512,512]{3,2,1,0:T(8,128)}, f32[1,2,512,512]{3,2,1,0:T(8,128)}) fusion(f32[2,2,512,512]{3,2,1,0:T(8,128)} %param.8), kind=kLoop, calls=%fused_computation.345 | loop fusion | bytes 8388608 | tf_op jit(solution)/shard_map/slice | solution.py:48
  69.0 1.9 copy.83
  71.0 2.9 %copy.84 = f32[1,2,512,512]{2,3,1,0:T(8,128)} copy(f32[1,2,512,512]{3,2,1,0:T(8,128)} %get-tuple-element.12) | data formatting | bytes 4194304
  73.9 4.0 %fusion.33 = bf16[1,512,512]{2,1,0:T(8,128)(2,1)S(1)} fusion(), kind=kLoop, calls=%fused_computation.176 | loop fusion | flops 3932160 | bytes 524288 | tf_op jit(solution)/shard_map/convert.13
  77.8 4.3 %negate_convert_fusion = (bf16[1,512,512]{2,1,0:T(8,128)(2,1)S(1)}, bf16[1,512,512]{2,1,0:T(8,128)(2,1)S(1)}) fusion(), kind=kLoop, calls=%fused_computation.165 | loop fusion | flops 4456448 | bytes 1048576 | tf_op jit(solution)/shard_map/convert.9
  82.2 1.5 maximum_bitcast_fusion.3
  83.7 0.2 fusion.116
  83.9 31.6 %all-to-all-done.2 = bf16[128,2,8,512]{3,2,1,0:T(8,128)(2,1)} async-done(((bf16[128,2,8,512]{3,2,1,0:T(8,128)(2,1)}), bf16[128,2,8,512]{3,2,1,0:T(8,128)(2,1)}, u32[]{:S(2)}, u32[]{:S(2)}) %all-to-all-start.2) | async-done | bytes 2097184 | tf_op jit(solution)/shard_map/all_to_all | solution.py:44
  115.5 4.7 %convolution_bitcast_fusion.1 = f32[2,2,512,512]{2,3,1,0:T(8,128)S(1)} fusion(bf16[2,2,64,8,512]{4,3,1,0,2:T(8,128)(2,1)} %bitcast.7, bf16[1,2,512,512]{3,2,1,0:T(8,128)(2,1)} %get-tuple-element.14, bf16[1,2,512,512]{3,2,1,0:T(8,128)(2,1)} %get-tuple-element.13), kind=kOutput, calls=%fused_computation.127 | convolution fusion | flops 2151677952 | bytes 8388608 | tf_op jit(solution)/shard_map/oisr,girc->gosc/dot_general | solution.py:18
  120.2 0.0 copy-done
  120.3 0.0 copy-start.1
  120.3 1.2 fusion.6
  121.5 0.3 copy-done.2
  121.8 2.5 %convolution_bitcast_fusion = f32[2,2,512,512]{3,2,1,0:T(8,128)S(1)} fusion(bf16[2,1,512,512]{2,3,1,0:T(8,128)(2,1)S(1)} %get-tuple-element.6, bf16[2,1,512,512]{2,3,1,0:T(8,128)(2,1)S(1)} %get-tuple-element.5, bf16[1,2,512,512]{3,2,1,0:T(8,128)(2,1)S(1)} %copy-done.2, bf16[1,2,512,512]{3,2,1,0:T(8,128)(2,1)S(1)} %copy-done.1), kind=kOutput, calls=%fused_computation.126 | convolution fusion | flops 2155872256 | bytes 8388608 | tf_op jit(solution)/shard_map/oisr,gosc->girc/dot_general | solution.py:18
  124.3 0.6 subtract_convert_fusion
  125.6 56.9 %all_to_all.74 = bf16[64,2,2,8,512]{4,3,2,1,0:T(8,128)(2,1)S(1)} all-to-all(bf16[64,2,2,8,512]{4,3,2,1,0:T(8,128)(2,1)S(1)} %constant_dynamic-update-slice_fusion), channel_id=1, replica_groups=mesh['seq'=64,'ch'=4] {'seq'}, dimensions={0} | all-to-all | bytes 4194304 | tf_op jit(solution)/shard_map/all_to_all | solution.py:59
  182.5 2.4 %fusion.18 = bf16[64,8,512]{2,0,1:T(8,128)(2,1)S(1)} fusion(bf16[128,2,8,512]{3,2,1,0:T(8,128)(2,1)S(1)} %bitcast.228, bf16[128,1,64]{0,2,1:T(8,128)(2,1)S(1)} %get-tuple-element.19, bf16[128,1,64]{0,2,1:T(8,128)(2,1)S(1)} %get-tuple-element.20), kind=kOutput, calls=%fused_computation.155 | convolution fusion | flops 134807552 | bytes 2654208 | tf_op jit(solution)/shard_map/kip,kirc->prc/dot_general | solution.py:18
  184.9 0.3 copy.66
  185.2 23.0 %all_to_all.75 = bf16[64,8,512]{2,1,0:T(8,128)(2,1)} all-to-all(bf16[64,8,512]{2,1,0:T(8,128)(2,1)S(1)} %copy.66), channel_id=1, replica_groups=mesh['seq'=64,'ch'=4] {'seq'}, dimensions={0} | all-to-all | bytes 1048576 | tf_op jit(solution)/shard_map/all_to_all | solution.py:65
  208.3 3.5 %all-to-all-start.5 = ((bf16[4,128,512]{2,1,0:T(8,128)(2,1)}), bf16[4,128,512]{2,1,0:T(8,128)(2,1)S(1)}, u32[]{:S(2)}, u32[]{:S(2)}) async-start(bf16[4,128,512]{2,1,0:T(8,128)(2,1)} %bitcast.92), calls=%async_computation.5 | async-start | bytes 1048576 | tf_op jit(solution)/shard_map/all_to_all | solution.py:73
  211.8 0.3 copy.52
  212.0 0.0 copy-start.4
  212.0 9.0 %all-to-all-done.5 = bf16[4,128,512]{2,1,0:T(8,128)(2,1)S(1)} async-done(((bf16[4,128,512]{2,1,0:T(8,128)(2,1)}), bf16[4,128,512]{2,1,0:T(8,128)(2,1)S(1)}, u32[]{:S(2)}, u32[]{:S(2)}) %all-to-all-start.5) | async-done | bytes 524320 | tf_op jit(solution)/shard_map/all_to_all | solution.py:73
  221.0 0.1 convert_bitcast_fusion
  221.1 0.3 copy.67
  221.5 0.0 copy-done.4
  221.5 0.3 fusion.25
  221.8 1.0 copy.68
  (71 shorter events, 0.3 us)
Async XLA Ops:
  22.5 30.7 %all-to-all-start.1 = ((bf16[64,2,2048]{2,1,0:T(2,128)(2,1)}), bf16[64,2,2048]{2,1,0:T(2,128)(2,1)S(1)}, u32[]{:S(2)}, u32[]{:S(2)}) async-start(bf16[64,2,2048]{2,1,0:T(2,128)(2,1)} %reshape.300), calls=%async_computation.1 | async-start | bytes 1048576 | tf_op jit(solution)/shard_map/all_to_all | solution.py:32
  57.9 57.6 %all-to-all-start.2 = ((bf16[128,2,8,512]{3,2,1,0:T(8,128)(2,1)}), bf16[128,2,8,512]{3,2,1,0:T(8,128)(2,1)}, u32[]{:S(2)}, u32[]{:S(2)}) async-start(bf16[128,2,8,512]{3,2,1,0:T(8,128)(2,1)} %copy.58), calls=%async_computation.2 | async-start | bytes 4194304 | tf_op jit(solution)/shard_map/all_to_all | solution.py:44
  115.5 4.7 %copy-start = (f32[1,2,512,512]{2,3,1,0:T(8,128)S(1)}, f32[1,2,512,512]{2,3,1,0:T(8,128)}, u32[]{:S(2)}) copy-start(f32[1,2,512,512]{2,3,1,0:T(8,128)} %copy.84) | copy-start | bytes 6291460
  120.3 1.2 copy-start.1
  120.3 1.5 copy-start.2
  184.9 26.8 %copy-start.3 = (bf16[128,2048]{1,0:T(8,128)(2,1)S(1)}, bf16[128,2048]{1,0:T(8,128)(2,1)}, u32[]{:S(2)}) copy-start(bf16[128,2048]{1,0:T(8,128)(2,1)} %param.5) | copy-start | bytes 1572868
  208.3 12.7 %all-to-all-start.5 = ((bf16[4,128,512]{2,1,0:T(8,128)(2,1)}), bf16[4,128,512]{2,1,0:T(8,128)(2,1)S(1)}, u32[]{:S(2)}, u32[]{:S(2)}) async-start(bf16[4,128,512]{2,1,0:T(8,128)(2,1)} %bitcast.92), calls=%async_computation.5 | async-start | bytes 1048576 | tf_op jit(solution)/shard_map/all_to_all | solution.py:73
  212.0 9.4 %copy-start.4 = (f32[2048]{0:T(1024)S(1)}, f32[2048]{0:T(1024)}, u32[]{:S(2)}) copy-start(f32[2048]{0:T(1024)} %param.9) | copy-start | bytes 24580
